TPU v7x, 512 devices: a whole 4x4x16 slice. The times are simulated.
512 devices in a mesh: len: 128 (over y, z, core), pipe: 4 (over x).
Axes of the slice: x: 4, y: 4, z: 16, core: 2. Of those that a mesh axis runs over, the one named last changes fastest.
Arguments:
- inputs: bfloat16 [512, 2048, 256], P(('len', 'pipe')), may hold values from -6 to 6
- cotangent: bfloat16 [512, 2048, 256], P(('len', 'pipe')), may hold values from -6 to 6
- point_weight: bfloat16 [256, 256], replicated, may hold values from -0.375 to 0.375
- point_bias: float32 [256], replicated, may hold values from -3 to 3
- spec_real: bfloat16 [128, 256, 256], P('len'), may hold values from -0.25 to 0.25
- spec_imag: bfloat16 [128, 256, 256], P('len'), may hold values from -0.25 to 0.25
- junc_weight: bfloat16 [256, 256], replicated, may hold values from -0.375 to 0.375
- junc_bias: float32 [256], replicated, may hold values from -3 to 3
- inlet_ids: int32 [512], replicated, may hold values from 0 to 511
- outlet_ids: int32 [512], replicated, may hold values from 0 to 511
Outputs:
- outputs: bfloat16 [512, 2048, 256], P(('len', 'pipe'))
- grad_inputs: bfloat16 [512, 2048, 256], P(('len', 'pipe'))
- grad_real: float32 [128, 256, 256], P('len')
- grad_imag: float32 [128, 256, 256], P('len')
All inputs are finite; a program needn't handle non-finite values.
Results may differ from a plain program's by a relative error of at most 0.015.
Values may be sent and summed in bfloat16 or wider, within the bound.
A program may use at most 64 MiB of HBM per device.

v0:
```python
import math
import jax
import jax.numpy as jnp
from jax import lax
from jax.sharding import PartitionSpec as P

COUPLING = 0.125


def tables(cell_count, mode_count):
    position = lax.broadcasted_iota(jnp.int32, (mode_count, cell_count), 1)
    frequency = lax.broadcasted_iota(jnp.int32, (mode_count, cell_count), 0)
    product_index = frequency * position % cell_count
    angles = product_index.astype(jnp.float32) * (2.0 * math.pi / cell_count)
    norm_scale = 1.0 / math.sqrt(cell_count)
    cosine = jnp.cos(angles) * norm_scale
    sine_table = jnp.sin(angles) * norm_scale
    doubled = jnp.where(frequency == 0, 1.0, 2.0)
    forward = (
        jnp.stack([cosine, -sine_table], axis=1)
        .reshape(2 * mode_count, cell_count)
        .astype(jnp.bfloat16)
    )
    inverse = jnp.transpose(
        jnp.stack([doubled * cosine, -doubled * sine_table], axis=1).reshape(
            2 * mode_count, cell_count
        )
    ).astype(jnp.bfloat16)
    return (forward, inverse)


def spectral_blocks(spec_real, spec_imag):
    upper = jnp.concatenate([spec_real, spec_imag], axis=2)
    lower = jnp.concatenate([-spec_imag, spec_real], axis=2)
    return jnp.concatenate([upper, lower], axis=1)


def activate(values):
    return jax.nn.gelu(values, approximate=True)


def silu_slope(values):
    sigmoid_part = jax.nn.sigmoid(values)
    return sigmoid_part * (1.0 + values * (1.0 - sigmoid_part))


def to_modes(field):
    return lax.all_to_all(field, "len", split_axis=1, concat_axis=0, tiled=True)


def from_modes(field):
    return lax.all_to_all(field, "len", split_axis=0, concat_axis=1, tiled=True)


def junction_pass(partial_value, rowwise, carried):
    summed_rows = lax.psum(partial_value, ("len", "pipe"))
    return rowwise(summed_rows, carried)


def body(
    inputs,
    cotangent,
    point_weight,
    point_bias,
    spec_real,
    spec_imag,
    junc_weight,
    junc_bias,
    inlet_ids,
    outlet_ids,
):
    per_dev, cell_count, channels = inputs.shape
    len_count = lax.axis_size("len")
    mode_count = spec_real.shape[0] * len_count
    junc_count = inlet_ids.shape[0]
    forward, inverse = tables(cell_count, mode_count)
    blocks = spectral_blocks(spec_real, spec_imag)
    start = (lax.axis_index("len") * lax.axis_size("pipe") + lax.axis_index("pipe")) * per_dev
    my_inlets = lax.dynamic_slice_in_dim(inlet_ids, start, per_dev)
    my_outlets = lax.dynamic_slice_in_dim(outlet_ids, start, per_dev)
    junction_iota = lax.broadcasted_iota(jnp.int32, (per_dev, junc_count), 1)
    in_hot = (my_inlets[:, None] == junction_iota).astype(jnp.bfloat16)
    out_hot = (my_outlets[:, None] == junction_iota).astype(jnp.bfloat16)
    spectra = jnp.einsum("kl,plc->pkc", forward, inputs, preferred_element_type=jnp.float32).astype(
        jnp.bfloat16
    )
    mode_rows = to_modes(spectra.reshape(per_dev, mode_count, 2, channels))
    mode_rows = mode_rows.reshape(mode_rows.shape[0], -1, 2 * channels)
    mixed = jnp.einsum(
        "pmk,mkn->pmn", mode_rows, blocks, preferred_element_type=jnp.float32
    ).astype(jnp.bfloat16)
    returned_modes = from_modes(mixed.reshape(mixed.shape[0], -1, 2, channels)).reshape(
        per_dev, 2 * mode_count, channels
    )

    def forward_rows(summed_rows, carried):
        junc_act = (
            jnp.dot(
                summed_rows.astype(jnp.bfloat16), junc_weight, preferred_element_type=jnp.float32
            )
            + junc_bias
        )
        return (jax.nn.silu(junc_act).astype(jnp.bfloat16), junc_act)

    def backward_rows(summed_rows, carried):
        act_grad = (summed_rows * silu_slope(carried)).astype(jnp.bfloat16)
        return (
            jnp.dot(act_grad, junc_weight.T, preferred_element_type=jnp.float32).astype(
                jnp.bfloat16
            ),
            carried,
        )

    partial_value = jnp.dot(
        in_hot.T, inputs[:, 0, :], preferred_element_type=jnp.float32
    ) + jnp.dot(out_hot.T, inputs[:, -1, :], preferred_element_type=jnp.float32)
    junc_rows, junc_act = junction_pass(partial_value, forward_rows, None)
    cond = COUPLING * (
        jnp.dot(in_hot, junc_rows, preferred_element_type=jnp.float32)
        + jnp.dot(out_hot, junc_rows, preferred_element_type=jnp.float32)
    )
    spectral = jnp.einsum(
        "lk,pkc->plc", inverse, returned_modes, preferred_element_type=jnp.float32
    )
    pre = (spectral + cond[:, None, :]).astype(jnp.bfloat16)
    pointwise = jnp.dot(
        inputs.reshape(-1, channels), point_weight, preferred_element_type=jnp.float32
    ).reshape(inputs.shape)
    summed = pointwise + point_bias + pre.astype(jnp.float32)
    result, pullback = jax.vjp(activate, summed)
    outputs = result.astype(jnp.bfloat16)
    grad_total = pullback(cotangent.astype(jnp.float32))[0].astype(jnp.bfloat16)
    grad_spec = jnp.einsum(
        "lk,plc->pkc", inverse, grad_total, preferred_element_type=jnp.float32
    ).astype(jnp.bfloat16)
    grad_modes = to_modes(grad_spec.reshape(per_dev, mode_count, 2, channels))
    grad_modes = grad_modes.reshape(grad_modes.shape[0], -1, 2 * channels)
    grad_mixed = jnp.einsum(
        "pmn,mkn->pmk", grad_modes, blocks, preferred_element_type=jnp.float32
    ).astype(jnp.bfloat16)
    weight_terms = jnp.einsum(
        "pmk,pmn->mkn", mode_rows, grad_modes, preferred_element_type=jnp.float32
    )
    real_terms = weight_terms[:, :channels, :channels] + weight_terms[:, channels:, channels:]
    imag_terms = weight_terms[:, :channels, channels:] - weight_terms[:, channels:, :channels]
    grad_real, grad_imag = (
        lax.psum(real_terms.astype(jnp.bfloat16), "pipe").astype(jnp.float32),
        lax.psum(imag_terms.astype(jnp.bfloat16), "pipe").astype(jnp.float32),
    )
    grad_back = from_modes(grad_mixed.reshape(grad_mixed.shape[0], -1, 2, channels)).reshape(
        per_dev, 2 * mode_count, channels
    )
    grad_cells = jnp.einsum("kl,pkc->plc", forward, grad_back, preferred_element_type=jnp.float32)
    grad_cond = jnp.sum(grad_total, axis=1, dtype=jnp.float32)
    in_wide = in_hot.astype(jnp.float32)
    out_wide = out_hot.astype(jnp.float32)
    partial_grad = COUPLING * (
        jnp.dot(in_wide.T, grad_cond, precision=lax.Precision.HIGHEST)
        + jnp.dot(out_wide.T, grad_cond, precision=lax.Precision.HIGHEST)
    )
    sums_grad, unused = junction_pass(partial_grad, backward_rows, junc_act)
    end_first = jnp.dot(in_hot, sums_grad, preferred_element_type=jnp.float32)
    end_last = jnp.dot(out_hot, sums_grad, preferred_element_type=jnp.float32)
    grad_cells = grad_cells.at[:, 0, :].add(end_first).at[:, -1, :].add(end_last)
    spread = grad_cells.astype(jnp.bfloat16)
    grad_local = jnp.dot(
        grad_total.reshape(-1, channels), point_weight.T, preferred_element_type=jnp.float32
    ).reshape(inputs.shape)
    grad_inputs = (grad_local + spread.astype(jnp.float32)).astype(jnp.bfloat16)
    return (outputs, grad_inputs, grad_real, grad_imag)


def solution(mesh):
    placed = (
        P(("len", "pipe"), None, None),
        P(("len", "pipe"), None, None),
        P(),
        P(),
        P("len", None, None),
        P("len", None, None),
        P(),
        P(),
        P(),
        P(),
    )
    return jax.shard_map(
        body,
        mesh=mesh,
        in_specs=placed,
        out_specs=(
            P(("len", "pipe"), None, None),
            P(("len", "pipe"), None, None),
            P("len", None, None),
            P("len", None, None),
        ),
        check_vma=False,
    )
```

profile of v0, /device:TPU:8, one launch (start us, length us, event | category | flops | bytes accessed | tf_op | source)
XLA Modules:
  0.0 741.6 jit_solution(12216176334191740046)
XLA Ops:
  7.2 4.3 negate_convert_fusion
  11.6 1.1 copy.32
  14.4 19.6 %all-to-all-start = ((bf16[1,128,2,256]{3,2,0,1:T(2,128)(2,1)}), bf16[1,128,2,256]{3,2,0,1:T(2,128)(2,1)S(1)}, u32[]{:S(2)}, u32[]{:S(2)}) async-start(bf16[1,128,2,256]{3,2,0,1:T(2,128)(2,1)} %bitcast.6), calls=%async_computation | async-start | bytes 262144 | tf_op jit(solution)/shard_map/all_to_all | solution.py:48
  34.0 1.3 dynamic_slice.6
  36.0 1.2 dynamic_slice.7
  38.0 106.2 %all-reduce.8 = bf16[512,256]{1,0:T(8,128)(2,1)S(1)} all-reduce(f32[512,256]{1,0:T(8,128)S(1)} %multiply_add_fusion), channel_id=1, replica_groups=mesh['len'=128,'pipe'=4] {'len','pipe'}, use_global_device_ids=true, to_apply=%region_0.1 | all-reduce | flops 131072 | bytes 786432 | tf_op jit(solution)/shard_map/psum | solution.py:56
  144.2 4.4 multiply_convert_fusion.1
  148.6 1.0 multiply_convert_fusion.5
  151.1 0.8 copy.34
  151.9 15.3 %all-to-all-start.1 = ((bf16[128,1,2,256]{3,2,1,0:T(2,128)(2,1)}), bf16[128,1,2,256]{3,2,1,0:T(2,128)(2,1)}, u32[]{:S(2)}, u32[]{:S(2)}) async-start(bf16[128,1,2,256]{3,2,1,0:T(2,128)(2,1)} %copy.34), calls=%async_computation.1 | async-start | bytes 262144 | tf_op jit(solution)/shard_map/all_to_all | solution.py:52
  167.8 1.1 copy.35
  169.5 14.5 %all-to-all-done.1 = bf16[128,1,2,256]{3,2,1,0:T(2,128)(2,1)} async-done(((bf16[128,1,2,256]{3,2,1,0:T(2,128)(2,1)}), bf16[128,1,2,256]{3,2,1,0:T(2,128)(2,1)}, u32[]{:S(2)}, u32[]{:S(2)}) %all-to-all-start.1) | async-done | bytes 131104 | tf_op jit(solution)/shard_map/all_to_all | solution.py:52
  184.1 1.0 reshape.386
  186.2 3.0 convert_reduce_fusion
  189.2 1.0 copy-done.1
  191.4 7.2 all-to-all-start.2
  198.7 1.2 convert_add_fusion
  199.9 1.0 multiply_multiply_fusion.2
  200.9 15.0 %all-to-all-done.2 = bf16[1,128,2,256]{3,2,0,1:T(2,128)(2,1)S(1)} async-done(((bf16[1,128,2,256]{3,2,0,1:T(2,128)(2,1)}), bf16[1,128,2,256]{3,2,0,1:T(2,128)(2,1)S(1)}, u32[]{:S(2)}, u32[]{:S(2)}) %all-to-all-start.2) | async-done | bytes 131104 | tf_op jit(solution)/shard_map/all_to_all | solution.py:48
  216.5 0.8 copy.38
  217.3 7.2 all-to-all-start.3
  225.3 439.5 %all-reduce.5.cloned.1.call-done = f32[512,256]{1,0:T(8,128)} async-done(((f32[512,256]{1,0:T(8,128)}), f32[512,256]{1,0:T(8,128)}) %all-reduce.5.cloned.1.call-update) | async-done | bytes 524304 | tf_op jit(solution)/shard_map/psum | solution.py:56
  664.8 1.4 convolution_convert_fusion
  666.4 54.7 %all-reduce.7.cloned.1.call-done = (bf16[1,256,256]{2,1,0:T(8,128)(2,1)}, bf16[1,256,256]{2,1,0:T(8,128)(2,1)}) async-done(((bf16[1,256,256]{2,1,0:T(8,128)(2,1)}, bf16[1,256,256]{2,1,0:T(8,128)(2,1)}), (bf16[1,256,256]{2,1,0:T(8,128)(2,1)}, bf16[1,256,256]{2,1,0:T(8,128)(2,1)})) %all-reduce.7.cloned.1.call-update) | async-done | bytes 262160 | tf_op jit(solution)/shard_map/psum | solution.py:147
  721.0 1.6 convert_element_type.176
  722.7 1.6 convert_element_type.178
  725.0 1.4 fusion.43
  726.5 1.8 copy.39
  728.3 1.3 scatter-add.6
  729.6 0.8 fusion.20
  730.4 1.3 scatter-add.9
  731.8 3.0 fusion.4
  (76 shorter events, 10.5 us)
Async XLA Ops:
  7.2 178.4 %copy-start = (bf16[256,256]{1,0:T(8,128)(2,1)S(1)}, bf16[256,256]{1,0:T(8,128)(2,1)}, u32[]{:S(2)}) copy-start(bf16[256,256]{1,0:T(8,128)(2,1)} %param.16) | copy-start | bytes 393220
  11.6 1.5 copy-start.3
  13.2 135.4 %copy-start.14 = (bf16[256,256]{1,0:T(8,128)(2,1)S(1)}, bf16[256,256]{1,0:T(8,128)(2,1)}, u32[]{:S(2)}) copy-start(bf16[256,256]{1,0:T(8,128)(2,1)} %param.20) | copy-start | bytes 393220
  13.2 135.4 %copy-start.16 = (f32[256]{0:T(256)S(1)}, f32[256]{0:T(256)}, u32[]{:S(2)}) copy-start(f32[256]{0:T(256)} %param.21) | copy-start | bytes 3076
  14.4 136.3 %all-to-all-start = ((bf16[1,128,2,256]{3,2,0,1:T(2,128)(2,1)}), bf16[1,128,2,256]{3,2,0,1:T(2,128)(2,1)S(1)}, u32[]{:S(2)}, u32[]{:S(2)}) async-start(bf16[1,128,2,256]{3,2,0,1:T(2,128)(2,1)} %bitcast.6), calls=%async_computation | async-start | bytes 262144 | tf_op jit(solution)/shard_map/all_to_all | solution.py:48
  144.2 6.1 copy-start.7
  149.7 1.0 copy-start.12
  150.4 0.7 copy-start.9
  150.7 17.1 %copy-start.5 = (bf16[16,8,2,256]{3,1,2,0:T(8,128)(2,1)}, bf16[16,8,2,256]{3,1,2,0:T(8,128)(2,1)S(1)}, u32[]{:S(2)}) copy-start(bf16[16,8,2,256]{3,1,2,0:T(8,128)(2,1)S(1)} %copy.41) | copy-start | bytes 393220
  151.9 32.2 %all-to-all-start.1 = ((bf16[128,1,2,256]{3,2,1,0:T(2,128)(2,1)}), bf16[128,1,2,256]{3,2,1,0:T(2,128)(2,1)}, u32[]{:S(2)}, u32[]{:S(2)}) async-start(bf16[128,1,2,256]{3,2,1,0:T(2,128)(2,1)} %copy.34), calls=%async_computation.1 | async-start | bytes 262144 | tf_op jit(solution)/shard_map/all_to_all | solution.py:52
  169.3 16.3 %copy-start.4 = (bf16[1,2048,256]{2,1,0:T(8,128)(2,1)S(1)}, bf16[1,2048,256]{2,1,0:T(8,128)(2,1)}, u32[]{:S(2)}) copy-start(bf16[1,2048,256]{2,1,0:T(8,128)(2,1)} %param.14) | copy-start | bytes 3145732
  169.3 16.3 %copy-start.17 = (f32[256]{0:T(256)S(1)}, f32[256]{0:T(256)}, u32[]{:S(2)}) copy-start(f32[256]{0:T(256)} %param.17) | copy-start | bytes 3076
  185.0 1.2 copy-start.11
  189.2 1.0 copy-start.1
  189.2 26.6 %copy-start.8 = (bf16[1,256,256]{2,1,0:T(8,128)(2,1)S(1)}, bf16[1,256,256]{2,1,0:T(8,128)(2,1)}, u32[]{:S(2)}) copy-start(bf16[1,256,256]{2,1,0:T(8,128)(2,1)} %param.19) | copy-start | bytes 393220
  189.2 26.6 %copy-start.10 = (bf16[1,256,256]{2,1,0:T(8,128)(2,1)S(1)}, bf16[1,256,256]{2,1,0:T(8,128)(2,1)}, u32[]{:S(2)}) copy-start(bf16[1,256,256]{2,1,0:T(8,128)(2,1)} %copy-done.9) | copy-start | bytes 393220
  189.2 26.6 %copy-start.13 = (bf16[1,256,256]{2,1,0:T(8,128)(2,1)S(1)}, bf16[1,256,256]{2,1,0:T(8,128)(2,1)}, u32[]{:S(2)}) copy-start(bf16[1,256,256]{2,1,0:T(8,128)(2,1)} %param.18) | copy-start | bytes 393220
  190.7 25.5 %copy-start.6 = (bf16[16,8,2,256]{3,1,2,0:T(8,128)(2,1)S(1)}, bf16[16,8,2,256]{3,1,2,0:T(8,128)(2,1)}, u32[]{:S(2)}) copy-start(bf16[16,8,2,256]{3,1,2,0:T(8,128)(2,1)} %copy-done.5) | copy-start | bytes 393220
  191.4 24.4 %all-to-all-start.2 = ((bf16[1,128,2,256]{3,2,0,1:T(2,128)(2,1)}), bf16[1,128,2,256]{3,2,0,1:T(2,128)(2,1)S(1)}, u32[]{:S(2)}, u32[]{:S(2)}) async-start(bf16[1,128,2,256]{3,2,0,1:T(2,128)(2,1)} %bitcast.24), calls=%async_computation.2 | async-start | bytes 262144 | tf_op jit(solution)/shard_map/all_to_all | solution.py:48
  198.6 466.2 %all-reduce.5.cloned.1.call-start = ((), (), s32[]{:S(2)}) async-start(), calls=%async_computation.4 | async-start | bytes 1048576 | tf_op jit(solution)/shard_map/psum | solution.py:56
  216.2 448.6 %copy-start.15 = (bf16[256,256]{1,0:T(8,128)(2,1)S(1)}, bf16[256,256]{1,0:T(8,128)(2,1)}, u32[]{:S(2)}) copy-start(bf16[256,256]{1,0:T(8,128)(2,1)} %param.20) | copy-start | bytes 393220
  216.2 448.6 %copy-start.18 = (f32[512,256]{1,0:T(8,128)S(1)}, f32[512,256]{1,0:T(8,128)}, u32[]{:S(2)}) copy-start(f32[512,256]{1,0:T(8,128)} %get-tuple-element.38) | copy-start | bytes 1572868
  217.3 507.0 %all-to-all-start.3 = ((bf16[128,1,2,256]{3,2,1,0:T(2,128)(2,1)}), bf16[128,1,2,256]{3,2,1,0:T(2,128)(2,1)S(1)}, u32[]{:S(2)}, u32[]{:S(2)}) async-start(bf16[128,1,2,256]{3,2,1,0:T(2,128)(2,1)} %copy.38), calls=%async_computation.3 | async-start | bytes 262144 | tf_op jit(solution)/shard_map/all_to_all | solution.py:52
  224.5 496.5 %all-reduce.7.cloned.1.call-start = ((), (), s32[]{:S(2)}) async-start(), calls=%async_computation.5 | async-start | bytes 524288 | tf_op jit(solution)/shard_map/psum | solution.py:147
  726.5 5.3 copy-start.2
Sparse Core Ops, SparseCore 0:
  204.9 459.8 all-reduce.4
  667.9 53.0 all-reduce.6
where the time goes:
time: 742 us
  waiting for transfers between devices  524 us (71%)
  blocking collectives  106 us (14%)
  starting transfers between devices  49.5 us (7%)
  other arithmetic  17.7 us (2%)
  local copies, waits for them, and re-layouts  16.5 us (2%)
  between operations  14.6 us (2%)
  matrix products  13.5 us (2%)
    psum x1, waiting for transfers between devices, junction_pass(): summed_rows = lax.psum(partial_value, ('len', 'pipe'))  439 us
    psum x1, blocking collectives, junction_pass(): summed_rows = lax.psum(partial_value, ('len', 'pipe'))  106 us
    psum x1, waiting for transfers between devices, body(): lax.psum(real_terms.astype(jnp.bfloat16), 'pipe').astype(jnp.float32)  54.7 us
    all_to_all x2, starting transfers between devices, to_modes(): return lax.all_to_all(field, 'len', split_axis=1, concat_axis=0, tiled=True)  26.8 us
    all_to_all x2, starting transfers between devices, from_modes(): return lax.all_to_all(field, 'len', split_axis=0, concat_axis=1, tiled=True)  22.5 us
    all_to_all x2, waiting for transfers between devices, to_modes(): return lax.all_to_all(field, 'len', split_axis=1, concat_axis=0, tiled=True)  15 us
  transfers between devices with their start and end apart: 6, of which 4 were waited for; matrix products, arithmetic and copies ran while one was open for 3% of the time, Pallas kernels for 0%

commit v1 on v0

--- a/solution.py
+++ b/solution.py
@@ -53,7 +53,9 @@
 
 
 def junction_pass(partial_value, rowwise, carried):
-    summed_rows = lax.psum(partial_value, ("len", "pipe"))
+    summed_rows = partial_value
+    for name in ("len", "pipe"):
+        summed_rows = lax.psum(summed_rows, name)
     return rowwise(summed_rows, carried)
 
 

time: 742 us -> 892 us (1.20)
  waiting for transfers between devices: 524 us -> 751 us
  blocking collectives: 106 us -> 23.2 us
    psum x1 -> x3, waiting for transfers between devices: 439 us -> 676 us  [junction_pass(): summed_rows = lax.psum(summed_rows, name)]
    psum x1, blocking collectives: 106 us -> 23.2 us  [junction_pass(): summed_rows = lax.psum(summed_rows, name)]
    psum x1, waiting for transfers between devices: 54.7 us -> 43.7 us  [body(): lax.psum(real_terms.astype(jnp.bfloat16), 'pipe').astype(jnp.float32)]
  transfers between devices with their start and end apart: 6 -> 8, of which waited for: 4 -> 6; matrix products, arithmetic and copies ran while one was open for 3% -> 3% of each run, Pallas kernels for 0% -> 0%
where the time goes in v1:
time: 892 us; the launch traced here: 891 us
  waiting for transfers between devices  751 us (84%)
  starting transfers between devices  51.6 us (6%)
  blocking collectives  23.2 us (3%)
  other arithmetic  20 us (2%)
  local copies, waits for them, and re-layouts  16.6 us (2%)
  matrix products  14.4 us (2%)
  between operations  14.2 us (2%)
    psum x3, waiting for transfers between devices, junction_pass(): summed_rows = lax.psum(summed_rows, name)  676 us
    psum x1, waiting for transfers between devices, body(): lax.psum(real_terms.astype(jnp.bfloat16), 'pipe').astype(jnp.float32)  43.7 us
    all_to_all x2, starting transfers between devices, to_modes(): return lax.all_to_all(field, 'len', split_axis=1, concat_axis=0, tiled=True)  26.8 us
    all_to_all x2, starting transfers between devices, from_modes(): return lax.all_to_all(field, 'len', split_axis=0, concat_axis=1, tiled=True)  24.6 us
    psum x1, blocking collectives, junction_pass(): summed_rows = lax.psum(summed_rows, name)  23.2 us
  transfers between devices with their start and end apart: 8, of which 6 were waited for; matrix products, arithmetic and copies ran while one was open for 3% of the time, Pallas kernels for 0%

profile of v1, /device:TPU:8, one launch (start us, length us, event | category | flops | bytes accessed | tf_op | source)
XLA Modules:
  0.0 891.1 jit_solution(5229595447584517091)
XLA Ops:
  7.2 1.3 dynamic_slice.6
  9.2 1.3 dynamic_slice.7
  11.9 1.0 multiply_add_fusion
  12.9 4.3 negate_convert_fusion
  17.3 1.1 copy.32
  20.1 19.6 %all-to-all-start = ((bf16[1,128,2,256]{3,2,0,1:T(2,128)(2,1)}), bf16[1,128,2,256]{3,2,0,1:T(2,128)(2,1)S(1)}, u32[]{:S(2)}, u32[]{:S(2)}) async-start(bf16[1,128,2,256]{3,2,0,1:T(2,128)(2,1)} %bitcast.6), calls=%async_computation | async-start | bytes 262144 | tf_op jit(solution)/shard_map/all_to_all | solution.py:48
  40.3 4.4 multiply_convert_fusion.1
  46.2 1.1 copy.35
  47.7 301.5 %all-reduce.7.cloned.1.call-done = f32[512,256]{1,0:T(8,128)} async-done(((f32[512,256]{1,0:T(8,128)}), f32[512,256]{1,0:T(8,128)}) %all-reduce.7.cloned.1.call-update) | async-done | bytes 524304 | tf_op jit(solution)/shard_map/psum | solution.py:58
  349.2 23.2 %all-reduce.14 = bf16[512,256]{1,0:T(8,128)(2,1)S(1)} all-reduce(f32[512,256]{1,0:T(8,128)} %all-reduce.7.cloned.1.call-done), channel_id=1, replica_groups=mesh['len'=128,'pipe'=4] {'pipe'}, use_global_device_ids=true, to_apply=%region_1.2 | all-reduce | flops 131072 | bytes 786432 | tf_op jit(solution)/shard_map/psum | solution.py:58
  372.5 1.9 multiply_convert_fusion.5
  375.6 12.5 %all-to-all-start.1 = ((bf16[128,1,2,256]{3,2,1,0:T(2,128)(2,1)}), bf16[128,1,2,256]{3,2,1,0:T(2,128)(2,1)}, u32[]{:S(2)}, u32[]{:S(2)}) async-start(bf16[128,1,2,256]{3,2,1,0:T(2,128)(2,1)} %copy.34), calls=%async_computation.1 | async-start | bytes 262144 | tf_op jit(solution)/shard_map/all_to_all | solution.py:52
  388.4 16.5 %all-to-all-done.1 = bf16[128,1,2,256]{3,2,1,0:T(2,128)(2,1)} async-done(((bf16[128,1,2,256]{3,2,1,0:T(2,128)(2,1)}), bf16[128,1,2,256]{3,2,1,0:T(2,128)(2,1)}, u32[]{:S(2)}, u32[]{:S(2)}) %all-to-all-start.1) | async-done | bytes 131104 | tf_op jit(solution)/shard_map/all_to_all | solution.py:52
  405.0 1.0 reshape.386
  407.2 3.0 convert_reduce_fusion
  410.2 1.0 copy-done.1
  412.3 7.2 all-to-all-start.2
  419.6 1.3 convert_add_fusion
  420.8 0.9 multiply_multiply_fusion.2
  421.9 14.9 %all-to-all-done.2 = bf16[1,128,2,256]{3,2,0,1:T(2,128)(2,1)S(1)} async-done(((bf16[1,128,2,256]{3,2,0,1:T(2,128)(2,1)}), bf16[1,128,2,256]{3,2,0,1:T(2,128)(2,1)S(1)}, u32[]{:S(2)}, u32[]{:S(2)}) %all-to-all-start.2) | async-done | bytes 131104 | tf_op jit(solution)/shard_map/all_to_all | solution.py:48
  437.9 316.4 %all-reduce.9.cloned.1.call-done = f32[512,256]{1,0:T(8,128)} async-done(((f32[512,256]{1,0:T(8,128)}), f32[512,256]{1,0:T(8,128)}) %all-reduce.9.cloned.1.call-update) | async-done | bytes 524304 | tf_op jit(solution)/shard_map/psum | solution.py:58
  755.4 12.1 %all-to-all-start.3 = ((bf16[128,1,2,256]{3,2,1,0:T(2,128)(2,1)}), bf16[128,1,2,256]{3,2,1,0:T(2,128)(2,1)S(1)}, u32[]{:S(2)}, u32[]{:S(2)}) async-start(bf16[128,1,2,256]{3,2,1,0:T(2,128)(2,1)} %copy.38), calls=%async_computation.3 | async-start | bytes 262144 | tf_op jit(solution)/shard_map/all_to_all | solution.py:52
  767.6 43.7 %all-reduce.13.cloned.1.call-done = (bf16[1,256,256]{2,1,0:T(8,128)(2,1)}, bf16[1,256,256]{2,1,0:T(8,128)(2,1)}) async-done(((bf16[1,256,256]{2,1,0:T(8,128)(2,1)}, bf16[1,256,256]{2,1,0:T(8,128)(2,1)}), (bf16[1,256,256]{2,1,0:T(8,128)(2,1)}, bf16[1,256,256]{2,1,0:T(8,128)(2,1)})) %all-reduce.13.cloned.1.call-update) | async-done | bytes 262160 | tf_op jit(solution)/shard_map/psum | solution.py:149
  811.3 1.6 convert_element_type.176
  812.9 1.6 convert_element_type.178
  814.5 58.0 %all-reduce.11.cloned.1.call-done = f32[512,256]{1,0:T(8,128)} async-done(((f32[512,256]{1,0:T(8,128)}), f32[512,256]{1,0:T(8,128)}) %all-reduce.11.cloned.1.call-update) | async-done | bytes 524304 | tf_op jit(solution)/shard_map/psum | solution.py:58
  872.6 1.4 convolution_convert_fusion
  874.8 1.4 fusion.43
  876.3 1.8 copy.39
  878.1 1.3 scatter-add.6
  880.3 1.3 scatter-add.9
  881.6 3.0 fusion.4
  (80 shorter events, 14.2 us)
Async XLA Ops:
  7.2 399.3 %copy-start = (bf16[256,256]{1,0:T(8,128)(2,1)S(1)}, bf16[256,256]{1,0:T(8,128)(2,1)}, u32[]{:S(2)}) copy-start(bf16[256,256]{1,0:T(8,128)(2,1)} %param.16) | copy-start | bytes 393220
  7.2 342.1 %all-reduce.7.cloned.1.call-start = ((), (), s32[]{:S(2)}) async-start(), calls=%async_computation.4 | async-start | bytes 1048576 | tf_op jit(solution)/shard_map/psum | solution.py:58
  17.3 1.5 copy-start.3
  18.9 26.5 %copy-start.7 = (bf16[1,256,256]{2,1,0:T(8,128)(2,1)S(1)}, bf16[1,256,256]{2,1,0:T(8,128)(2,1)}, u32[]{:S(2)}) copy-start(bf16[1,256,256]{2,1,0:T(8,128)(2,1)} %param.19) | copy-start | bytes 393220
  20.1 354.4 %all-to-all-start = ((bf16[1,128,2,256]{3,2,0,1:T(2,128)(2,1)}), bf16[1,128,2,256]{3,2,0,1:T(2,128)(2,1)S(1)}, u32[]{:S(2)}, u32[]{:S(2)}) async-start(bf16[1,128,2,256]{3,2,0,1:T(2,128)(2,1)} %bitcast.6), calls=%async_computation | async-start | bytes 262144 | tf_op jit(solution)/shard_map/all_to_all | solution.py:48
  46.2 326.3 %copy-start.15 = (f32[256]{0:T(256)S(1)}, f32[256]{0:T(256)}, u32[]{:S(2)}) copy-start(f32[256]{0:T(256)} %param.21) | copy-start | bytes 3076
  47.7 326.8 %copy-start.9 = (bf16[1,256,256]{2,1,0:T(8,128)(2,1)S(1)}, bf16[1,256,256]{2,1,0:T(8,128)(2,1)}, u32[]{:S(2)}) copy-start(bf16[1,256,256]{2,1,0:T(8,128)(2,1)} %neg.22) | copy-start | bytes 393220
  47.7 326.7 %copy-start.12 = (bf16[1,256,256]{2,1,0:T(8,128)(2,1)S(1)}, bf16[1,256,256]{2,1,0:T(8,128)(2,1)}, u32[]{:S(2)}) copy-start(bf16[1,256,256]{2,1,0:T(8,128)(2,1)} %param.18) | copy-start | bytes 393220
  374.5 1.2 copy-start.5
  375.6 29.3 %all-to-all-start.1 = ((bf16[128,1,2,256]{3,2,1,0:T(2,128)(2,1)}), bf16[128,1,2,256]{3,2,1,0:T(2,128)(2,1)}, u32[]{:S(2)}, u32[]{:S(2)}) async-start(bf16[128,1,2,256]{3,2,1,0:T(2,128)(2,1)} %copy.34), calls=%async_computation.1 | async-start | bytes 262144 | tf_op jit(solution)/shard_map/all_to_all | solution.py:52
  388.1 18.4 %copy-start.4 = (bf16[1,2048,256]{2,1,0:T(8,128)(2,1)S(1)}, bf16[1,2048,256]{2,1,0:T(8,128)(2,1)}, u32[]{:S(2)}) copy-start(bf16[1,2048,256]{2,1,0:T(8,128)(2,1)} %param.14) | copy-start | bytes 3145732
  388.1 18.4 %copy-start.16 = (f32[256]{0:T(256)S(1)}, f32[256]{0:T(256)}, u32[]{:S(2)}) copy-start(f32[256]{0:T(256)} %param.17) | copy-start | bytes 3076
  405.9 1.2 copy-start.11
  410.2 1.0 copy-start.1
  410.2 26.6 %copy-start.6 = (bf16[16,8,2,256]{3,1,2,0:T(8,128)(2,1)S(1)}, bf16[16,8,2,256]{3,1,2,0:T(8,128)(2,1)}, u32[]{:S(2)}) copy-start(bf16[16,8,2,256]{3,1,2,0:T(8,128)(2,1)} %copy-done.5) | copy-start | bytes 393220
  412.3 24.4 %all-to-all-start.2 = ((bf16[1,128,2,256]{3,2,0,1:T(2,128)(2,1)}), bf16[1,128,2,256]{3,2,0,1:T(2,128)(2,1)S(1)}, u32[]{:S(2)}, u32[]{:S(2)}) async-start(bf16[1,128,2,256]{3,2,0,1:T(2,128)(2,1)} %bitcast.24), calls=%async_computation.2 | async-start | bytes 262144 | tf_op jit(solution)/shard_map/all_to_all | solution.py:48
  419.5 334.7 %all-reduce.9.cloned.1.call-start = ((), (), s32[]{:S(2)}) async-start(), calls=%async_computation.5 | async-start | bytes 1048576 | tf_op jit(solution)/shard_map/psum | solution.py:58
  421.8 332.5 %copy-start.8 = (bf16[1,256,256]{2,1,0:T(8,128)(2,1)S(1)}, bf16[1,256,256]{2,1,0:T(8,128)(2,1)}, u32[]{:S(2)}) copy-start(bf16[1,256,256]{2,1,0:T(8,128)(2,1)} %param.19) | copy-start | bytes 393220
  421.8 332.5 %copy-start.10 = (bf16[1,256,256]{2,1,0:T(8,128)(2,1)S(1)}, bf16[1,256,256]{2,1,0:T(8,128)(2,1)}, u32[]{:S(2)}) copy-start(bf16[1,256,256]{2,1,0:T(8,128)(2,1)} %neg.22) | copy-start | bytes 393220
  421.8 332.5 %copy-start.13 = (bf16[1,256,256]{2,1,0:T(8,128)(2,1)S(1)}, bf16[1,256,256]{2,1,0:T(8,128)(2,1)}, u32[]{:S(2)}) copy-start(bf16[1,256,256]{2,1,0:T(8,128)(2,1)} %param.18) | copy-start | bytes 393220
  421.8 389.5 %all-reduce.13.cloned.1.call-start = ((), (), s32[]{:S(2)}) async-start(), calls=%async_computation.7 | async-start | bytes 524288 | tf_op jit(solution)/shard_map/psum | solution.py:149
  437.8 434.7 %copy-start.14 = (bf16[256,256]{1,0:T(8,128)(2,1)S(1)}, bf16[256,256]{1,0:T(8,128)(2,1)}, u32[]{:S(2)}) copy-start(bf16[256,256]{1,0:T(8,128)(2,1)} %param.20) | copy-start | bytes 393220
  437.8 434.7 %copy-start.17 = (f32[512,256]{1,0:T(8,128)S(1)}, f32[512,256]{1,0:T(8,128)}, u32[]{:S(2)}) copy-start(f32[512,256]{1,0:T(8,128)} %get-tuple-element.38) | copy-start | bytes 1572868
  437.9 434.7 %all-reduce.11.cloned.1.call-start = ((), (), s32[]{:S(2)}) async-start(), calls=%async_computation.6 | async-start | bytes 1048576 | tf_op jit(solution)/shard_map/psum | solution.py:58
  755.4 118.7 %all-to-all-start.3 = ((bf16[128,1,2,256]{3,2,1,0:T(2,128)(2,1)}), bf16[128,1,2,256]{3,2,1,0:T(2,128)(2,1)S(1)}, u32[]{:S(2)}, u32[]{:S(2)}) async-start(bf16[128,1,2,256]{3,2,1,0:T(2,128)(2,1)} %copy.38), calls=%async_computation.3 | async-start | bytes 262144 | tf_op jit(solution)/shard_map/all_to_all | solution.py:52
  876.3 5.3 copy-start.2
Sparse Core Ops, SparseCore 0:
  13.0 336.1 all-reduce.6
  424.2 330.0 all-reduce.8
  757.3 53.9 all-reduce.12
  813.6 58.8 all-reduce.10
